TPU v7x, 512 devices: a whole 4x8x8 slice. The times are simulated.
512 devices in a mesh: kpt: 16 (over x, y_hi), occ: 32 (over y_lo, z, core).
Axes of the slice: x: 4, y: 8 (y_hi: 4, y_lo: 2; y = y_hi * 2 + y_lo), z: 8, core: 2. Of those that a mesh axis runs over, the one named last changes fastest.
Arguments:
- factor: bfloat16 [2, 32, 32, 2, 256, 512], P(None, 'kpt', 'occ'), may hold values from -1.0546875 to 1.0546875
- partner: int32 [2, 32], replicated, may hold values from 0 to 31, as said below
- occ_energy: float32 [32, 32], replicated, may hold values from -3 to -0.5
- vir_sorted: float32 [32, 256], replicated, may hold values from 0.3 to 4.3, as said below
- vir_order: int32 [32, 256], replicated, may hold values from 0 to 255, each once within a row
Outputs:
- gradient_factor: bfloat16 [2, 32, 32, 2, 256, 512], P(None, 'kpt', 'occ')
Inputs may be any that keep to these rules, and one draw needn't show every extreme that they name: With group g holding k-points g * 2 to (g + 1) * 2 - 1, partner[0, k] lies in group (k // 2) XOR 1 and partner[1, k] in group (k // 2) XOR 8; which k-point of that group is arbitrary, and several k-points may share one. `vir_sorted`: each row is ascending and begins with 0.3.
All inputs are finite; a program needn't handle non-finite values.
Results may differ from a plain program's by a relative error of at most 0.0037.
Values may be sent and summed in bfloat16 or wider, within the bound.
A program may use at most 64 MiB of HBM per device.

v0:
```python
import jax
import jax.numpy as jnp
from jax import lax
from jax.sharding import PartitionSpec as P

REACH = 1


def padded(cells, sides, width):
    for axis, dim in sides:
        count = lax.axis_size(axis)
        head = lax.slice_in_dim(cells, 0, width, axis=dim)
        tail = lax.slice_in_dim(cells, cells.shape[dim] - width, cells.shape[dim], axis=dim)
        cells = jnp.concatenate(
            [
                lax.ppermute(tail, axis, [(i, (i + 1) % count) for i in range(count)]),
                cells,
                lax.ppermute(head, axis, [((i + 1) % count, i) for i in range(count)]),
            ],
            axis=dim,
        )
    return cells


def swapped(block, axis, distance):
    count = lax.axis_size(axis)
    route = []
    for low in range(count):
        high = low | 1 << distance
        if high != low and high < count:
            route += [(low, high), (high, low)]
    return lax.ppermute(block, axis, route)


def pick_rows(table, indices):
    matches = indices[:, None] == jnp.arange(table.shape[0], dtype=jnp.int32)[None, :]
    return jnp.sum(jnp.where(matches[:, :, None], table[None, :, :], 0), axis=1)


def pick_columns(rows, indices):
    matches = indices[:, None] == jnp.arange(rows.shape[1], dtype=jnp.int32)[None, :]
    return jnp.sum(jnp.where(matches[None, :, :], rows[:, None, :], 0), axis=2)


def virtual_rows(vir_sorted, vir_order, indices):
    levels = pick_rows(vir_sorted, indices)
    ranks = pick_rows(vir_order, indices)
    matches = ranks[:, :, None] == jnp.arange(vir_sorted.shape[1], dtype=jnp.int32)[None, None, :]
    return jnp.sum(jnp.where(matches, levels[:, None, :], 0.0), axis=2)


def body(factor, partner, occ_energy, vir_sorted, vir_order):
    transfers = factor.shape[0]
    kpt_count = factor.shape[1]
    occ_count = factor.shape[2]
    orbital_total = occ_energy.shape[1]
    group_id = lax.axis_index("kpt")
    orbit_id = lax.axis_index("occ")
    kpt_ids = group_id * kpt_count + jnp.arange(kpt_count, dtype=jnp.int32)
    occ_ids = orbit_id * occ_count + jnp.arange(occ_count, dtype=jnp.int32)
    top_bit = lax.axis_size("kpt").bit_length() - 2
    flip_bits = [0, top_bit]
    own_virtual = virtual_rows(vir_sorted, vir_order, kpt_ids)
    own_occupied = pick_columns(pick_rows(occ_energy, kpt_ids), occ_ids)

    def fetch_window(transfer):
        flip_bit = flip_bits[transfer]
        partner_group = jnp.bitwise_xor(group_id, 1 << flip_bit)
        partner_ids = pick_rows(partner[transfer][:, None], kpt_ids)[:, 0]
        slot_ids = partner_ids - partner_group * kpt_count
        own_block = factor[transfer]
        extended = padded(own_block, (("occ", 1),), REACH)
        extended = swapped(extended, "kpt", flip_bit)
        extended = jnp.take(extended, slot_ids, axis=0)
        return (extended, partner_ids)

    def contract_window(transfer, fetched):
        extended, partner_ids = fetched
        own_block = factor[transfer]
        rotated = jnp.stack([own_block[:, :, 1], -own_block[:, :, 0]], axis=2)
        stacked = jnp.stack([own_block, rotated], axis=2)
        partner_virtual = virtual_rows(vir_sorted, vir_order, partner_ids)
        partner_rows = pick_rows(occ_energy, partner_ids)
        gradient = jnp.zeros(own_block.shape, jnp.float32)
        for offset in range(-REACH, REACH + 1):
            window = extended[:, REACH + offset : REACH + offset + occ_count]
            pair_ints = jnp.einsum(
                "kircaq,kicbq->kirab", stacked, window, preferred_element_type=jnp.float32
            )
            columns = jnp.remainder(occ_ids + offset, orbital_total)
            partner_occ = pick_columns(partner_rows, columns)
            denominator = (
                own_occupied[:, :, None, None]
                + partner_occ[:, :, None, None]
                - partner_virtual[:, None, :, None]
                - own_virtual[:, None, None, :]
            )
            amplitude = (pair_ints / denominator[:, :, None]).astype(jnp.bfloat16)
            real_part = amplitude[:, :, 0]
            imag_part = amplitude[:, :, 1]
            combined = jnp.stack(
                [
                    jnp.stack([real_part, -imag_part], axis=2),
                    jnp.stack([imag_part, real_part], axis=2),
                ],
                axis=2,
            )
            gradient = gradient + jnp.einsum(
                "kixcab,kicbq->kixaq", combined, window, preferred_element_type=jnp.float32
            )
        return gradient.astype(jnp.bfloat16)

    results = [contract_window(transfer, fetch_window(transfer)) for transfer in range(transfers)]
    return jnp.stack(results, axis=0)


def solution(mesh):
    in_specs = (P(None, "kpt", "occ", None, None, None), P(), P(), P(), P())
    out_specs = P(None, "kpt", "occ", None, None, None)
    return jax.shard_map(body, mesh=mesh, in_specs=in_specs, out_specs=out_specs, check_vma=False)
```

profile of v0, /device:TPU:6, one launch (start us, length us, event | category | flops | bytes accessed | tf_op | source)
XLA Modules:
  0.0 201.8 jit_solution(17938722085538991358)
XLA Ops:
  0.0 3.4 %slice_bitcast_fusion.21 = (bf16[2,1,1,2,256,512]{5,4,3,2,0,1:T(8,128)(2,1)}, bf16[2,1,2,256,512]{4,3,2,0,1:T(8,128)(2,1)S(1)}, bf16[2,1,2,256,512]{4,3,2,0,1:T(8,128)(2,1)S(1)}, bf16[2,1,1,2,256,512]{5,4,3,2,0,1:T(8,128)(2,1)}) fusion(bf16[2,2,1,2,256,512]{5,4,3,1,2,0:T(8,128)(2,1)} %bitcast.260), kind=kLoop, calls=%fused_computation.68 | loop fusion | bytes 6291456 | tf_op jit(solution)/shard_map/stack;squeeze | solution.py:81
  3.4 1.9 collective-permute-start
  5.3 11.4 %collective-permute-start.1 = (bf16[2,1,2,256,512]{4,3,2,0,1:T(8,128)(2,1)S(1)}, bf16[2,1,2,256,512]{4,3,2,0,1:T(8,128)(2,1)}, u32[]{:S(2)}, u32[]{:S(2)}) collective-permute-start(bf16[2,1,2,256,512]{4,3,2,0,1:T(8,128)(2,1)S(1)} %get-tuple-element.31), channel_id=1, source_target_pairs={{1,0},{2,1},{3,2},{4,3},{5,4},{6,5},{7,6},{8,7},{9,8},{10,9},{11,1... | collective-permute-start | bytes 3145736 | tf_op jit(solution)/shard_map/ppermute | solution.py:18
  16.7 1.9 collective-permute-start.3
  18.7 5.8 %collective-permute-start.4 = (bf16[2,1,2,256,512]{4,3,2,0,1:T(8,128)(2,1)S(1)}, bf16[2,1,2,256,512]{4,3,2,0,1:T(8,128)(2,1)}, u32[]{:S(2)}, u32[]{:S(2)}) collective-permute-start(bf16[2,1,2,256,512]{4,3,2,0,1:T(8,128)(2,1)S(1)} %get-tuple-element.32), channel_id=1, source_target_pairs={{1,0},{2,1},{3,2},{4,3},{5,4},{6,5},{7,6},{8,7},{9,8},{10,9},{11,1... | collective-permute-start | bytes 3145736 | tf_op jit(solution)/shard_map/ppermute | solution.py:18
  25.2 2.1 %collective-permute-done = bf16[2,1,2,256,512]{4,3,2,0,1:T(8,128)(2,1)} collective-permute-done((bf16[2,1,2,256,512]{4,3,2,0,1:T(8,128)(2,1)S(1)}, bf16[2,1,2,256,512]{4,3,2,0,1:T(8,128)(2,1)}, u32[]{:S(2)}, u32[]{:S(2)}) %collective-permute-start) | collective-permute-done | bytes 1048608 | tf_op jit(solution)/shard_map/ppermute | solution.py:16
  27.4 1.7 collective-permute-done.1
  29.0 3.6 %pad_maximum_fusion = bf16[2,3,2,256,512]{4,3,2,0,1:T(8,128)(2,1)} fusion(bf16[2,1,2,256,512]{4,3,2,0,1:T(8,128)(2,1)} %collective-permute-done.1, bf16[2,1,2,256,512]{4,3,2,0,1:T(8,128)(2,1)S(1)} %get-tuple-element.31, bf16[2,1,2,256,512]{4,3,2,0,1:T(8,128)(2,1)} %collective-permute-done), kind=kLoop, calls=%fused_computation.2 | loop fusion | flops 3145728 | bytes 6291456 | tf_op jit(solution)/shard_map/concatenate | solution.py:14
  32.6 4.5 %collective-permute-start.2 = (bf16[2,3,2,256,512]{4,3,2,0,1:T(8,128)(2,1)}, bf16[2,3,2,256,512]{4,3,2,0,1:T(8,128)(2,1)}, u32[]{:S(2)}, u32[]{:S(2)}) collective-permute-start(bf16[2,3,2,256,512]{4,3,2,0,1:T(8,128)(2,1)} %pad_maximum_fusion), channel_id=1, source_target_pairs={{0,32},{32,0},{64,96},{96,64},{128,160},{160,128},{192,224},{224,1... | collective-permute-start | bytes 9437192 | tf_op jit(solution)/shard_map/ppermute | solution.py:32
  37.5 0.3 select_reduce_fusion.2
  37.7 0.3 select_reduce_fusion
  38.0 0.3 select_reduce_fusion.1
  38.4 1.1 maximum_bitcast_fusion.3
  39.5 1.1 maximum_bitcast_fusion.7
  40.6 7.3 %collective-permute-done.4 = bf16[2,1,2,256,512]{4,3,2,0,1:T(8,128)(2,1)} collective-permute-done((bf16[2,1,2,256,512]{4,3,2,0,1:T(8,128)(2,1)S(1)}, bf16[2,1,2,256,512]{4,3,2,0,1:T(8,128)(2,1)}, u32[]{:S(2)}, u32[]{:S(2)}) %collective-permute-start.4) | collective-permute-done | bytes 1048608 | tf_op jit(solution)/shard_map/ppermute | solution.py:18
  47.8 3.2 %pad_maximum_fusion.1 = bf16[2,3,2,256,512]{4,3,2,0,1:T(8,128)(2,1)} fusion(bf16[2,1,2,256,512]{4,3,2,0,1:T(8,128)(2,1)} %collective-permute-done.4, bf16[2,1,2,256,512]{4,3,2,0,1:T(8,128)(2,1)S(1)} %get-tuple-element.32, bf16[2,1,2,256,512]{4,3,2,0,1:T(8,128)(2,1)S(1)} %collective-permute-done.3), kind=kLoop, calls=%fused_computation.3 | loop fusion | flops 3145728 | bytes 6291456 | tf_op jit(solution)/shard_map/concatenate | solution.py:14
  51.1 3.5 %collective-permute-start.5 = (bf16[2,3,2,256,512]{4,3,2,0,1:T(8,128)(2,1)}, bf16[2,3,2,256,512]{4,3,2,0,1:T(8,128)(2,1)}, u32[]{:S(2)}, u32[]{:S(2)}) collective-permute-start(bf16[2,3,2,256,512]{4,3,2,0,1:T(8,128)(2,1)} %pad_maximum_fusion.1), channel_id=1, source_target_pairs={{0,256},{256,0},{32,288},{288,32},{64,320},{320,64},{96,352},{352,... | collective-permute-start | bytes 9437192 | tf_op jit(solution)/shard_map/ppermute | solution.py:32
  54.7 2.1 %broadcast_subtract_fusion.3 = (f32[2,256,256]{2,1,0:T(8,128)}, f32[2,256,256]{2,1,0:T(8,128)}, f32[2,256,256]{2,1,0:T(8,128)}, f32[2,256,256]{2,1,0:T(8,128)}, ...) fusion(f32[2,256]{1,0:T(2,128)S(1)} %get-tuple-element.74, f32[2,256]{1,0:T(2,128)S(1)} %select_reduce_fusion.1, ...), kind=kLoop, calls=%fused_computation.92 | loop fusion | flops 786432 | bytes 3160064 | tf_op jit(solution)/shard_map/sub | solution.py:93
  56.8 111.7 %collective-permute-done.2 = bf16[2,3,2,256,512]{4,3,2,0,1:T(8,128)(2,1)} collective-permute-done((bf16[2,3,2,256,512]{4,3,2,0,1:T(8,128)(2,1)}, bf16[2,3,2,256,512]{4,3,2,0,1:T(8,128)(2,1)}, u32[]{:S(2)}, u32[]{:S(2)}) %collective-permute-start.2) | collective-permute-done | bytes 3145760 | tf_op jit(solution)/shard_map/ppermute | solution.py:32
  168.5 3.8 %copy.34 = bf16[2,3,2,256,512]{4,3,2,1,0:T(8,128)(2,1)} copy(bf16[2,3,2,256,512]{4,3,2,0,1:T(8,128)(2,1)} %collective-permute-done.2) | data formatting | bytes 6291456 | tf_op jit(solution)/shard_map/ppermute | solution.py:32
  172.2 2.6 %gather_fusion = bf16[2,3,2,256,512]{4,3,2,1,0:T(8,128)(2,1)S(1)} fusion(bf16[2,3,2,256,512]{4,3,2,1,0:T(8,128)(2,1)} %copy.34, s32[1024]{0:T(1024)S(1)} %pad_clamp_fusion.1), kind=kCustom, calls=%fused_computation.clone | custom fusion | bytes 6291464 | tf_op jit(solution)/shard_map/jit(_take)/gather | solution.py:74
  174.9 0.4 copy_select_fusion.1
  175.3 0.8 copy-done.11
  176.1 0.8 copy-done.13
  177.0 0.5 copy-done.19
  177.5 0.7 fusion.12
  178.2 0.9 slice_negate_fusion.5
  179.1 0.7 fusion.6
  179.9 0.9 slice_negate_fusion.7
  180.8 0.7 fusion.9
  181.5 0.9 slice_negate_fusion.6
  182.4 3.8 %copy.41 = bf16[2,3,2,256,512]{4,3,2,1,0:T(8,128)(2,1)} copy(bf16[2,3,2,256,512]{4,3,2,0,1:T(8,128)(2,1)} %collective-permute-done.5) | data formatting | bytes 6291456 | tf_op jit(solution)/shard_map/ppermute | solution.py:32
  186.2 2.6 %gather_fusion.1 = bf16[2,3,2,256,512]{4,3,2,1,0:T(8,128)(2,1)S(1)} fusion(bf16[2,3,2,256,512]{4,3,2,1,0:T(8,128)(2,1)} %copy.41, s32[1024]{0:T(1024)S(1)} %pad_clamp_fusion), kind=kCustom, calls=%fused_computation.1.clone | custom fusion | bytes 6291464 | tf_op jit(solution)/shard_map/jit(_take)/gather | solution.py:74
  188.9 0.4 copy_select_fusion
  189.2 0.8 copy-done.10
  190.1 0.3 copy-done.12
  190.5 0.7 fusion.21
  191.3 0.2 copy-done.15
  191.6 0.7 fusion.15
  192.6 0.7 fusion.18
  193.8 1.5 copy-done.1
  195.3 0.7 fusion.30
  196.1 0.7 fusion.28
  196.9 0.7 fusion.25
  197.7 0.7 fusion.23
  198.8 0.7 fusion.2
  199.6 0.7 fusion.3
  200.3 1.5 maximum_bitcast_fusion.2
  (73 shorter events, 2.9 us)
Async XLA Ops:
  0.0 24.5 %copy-start.23 = (s32[2,32]{1,0:T(2,128)S(1)}, s32[2,32]{1,0:T(2,128)}, u32[]{:S(2)}) copy-start(s32[2,32]{1,0:T(2,128)} %param.8) | copy-start | bytes 772
  0.0 24.9 %copy-start.22 = (f32[32,32]{1,0:T(8,128)S(1)}, f32[32,32]{1,0:T(8,128)}, u32[]{:S(2)}) copy-start(f32[32,32]{1,0:T(8,128)} %param.9) | copy-start | bytes 12292
  3.4 24.0 %collective-permute-start = (bf16[2,1,2,256,512]{4,3,2,0,1:T(8,128)(2,1)S(1)}, bf16[2,1,2,256,512]{4,3,2,0,1:T(8,128)(2,1)}, u32[]{:S(2)}, u32[]{:S(2)}) collective-permute-start(bf16[2,1,2,256,512]{4,3,2,0,1:T(8,128)(2,1)S(1)} %get-tuple-element.31), channel_id=1, source_target_pairs={{0,1},{1,2},{2,3},{3,4},{4,5},{5,6},{6,7},{7,8},{8,9},{9,10},{10,1... | collective-permute-start | bytes 3145736 | tf_op jit(solution)/shard_map/ppermute | solution.py:16
  5.3 23.7 %collective-permute-start.1 = (bf16[2,1,2,256,512]{4,3,2,0,1:T(8,128)(2,1)S(1)}, bf16[2,1,2,256,512]{4,3,2,0,1:T(8,128)(2,1)}, u32[]{:S(2)}, u32[]{:S(2)}) collective-permute-start(bf16[2,1,2,256,512]{4,3,2,0,1:T(8,128)(2,1)S(1)} %get-tuple-element.31), channel_id=1, source_target_pairs={{1,0},{2,1},{3,2},{4,3},{5,4},{6,5},{7,6},{8,7},{9,8},{10,9},{11,1... | collective-permute-start | bytes 3145736 | tf_op jit(solution)/shard_map/ppermute | solution.py:18
  16.7 23.8 %collective-permute-start.3 = (bf16[2,1,2,256,512]{4,3,2,0,1:T(8,128)(2,1)S(1)}, bf16[2,1,2,256,512]{4,3,2,0,1:T(8,128)(2,1)S(1)}, u32[]{:S(2)}, u32[]{:S(2)}) collective-permute-start(bf16[2,1,2,256,512]{4,3,2,0,1:T(8,128)(2,1)S(1)} %get-tuple-element.32), channel_id=1, source_target_pairs={{0,1},{1,2},{2,3},{3,4},{4,5},{5,6},{6,7},{7,8},{8,9},{9,10},{10,1... | collective-permute-start | bytes 3145736 | tf_op jit(solution)/shard_map/ppermute | solution.py:16
  18.7 29.2 %collective-permute-start.4 = (bf16[2,1,2,256,512]{4,3,2,0,1:T(8,128)(2,1)S(1)}, bf16[2,1,2,256,512]{4,3,2,0,1:T(8,128)(2,1)}, u32[]{:S(2)}, u32[]{:S(2)}) collective-permute-start(bf16[2,1,2,256,512]{4,3,2,0,1:T(8,128)(2,1)S(1)} %get-tuple-element.32), channel_id=1, source_target_pairs={{1,0},{2,1},{3,2},{4,3},{5,4},{6,5},{7,6},{8,7},{9,8},{10,9},{11,1... | collective-permute-start | bytes 3145736 | tf_op jit(solution)/shard_map/ppermute | solution.py:18
  25.2 12.0 %copy-start.20 = (s32[32,256]{1,0:T(8,128)S(1)}, s32[32,256]{1,0:T(8,128)}, u32[]{:S(2)}) copy-start(s32[32,256]{1,0:T(8,128)} %param.11) | copy-start | bytes 98308
  25.2 12.1 %copy-start.21 = (f32[32,256]{1,0:T(8,128)S(1)}, f32[32,256]{1,0:T(8,128)}, u32[]{:S(2)}) copy-start(f32[32,256]{1,0:T(8,128)} %param.10) | copy-start | bytes 98308
  32.6 135.9 %collective-permute-start.2 = (bf16[2,3,2,256,512]{4,3,2,0,1:T(8,128)(2,1)}, bf16[2,3,2,256,512]{4,3,2,0,1:T(8,128)(2,1)}, u32[]{:S(2)}, u32[]{:S(2)}) collective-permute-start(bf16[2,3,2,256,512]{4,3,2,0,1:T(8,128)(2,1)} %pad_maximum_fusion), channel_id=1, source_target_pairs={{0,32},{32,0},{64,96},{96,64},{128,160},{160,128},{192,224},{224,1... | collective-permute-start | bytes 9437192 | tf_op jit(solution)/shard_map/ppermute | solution.py:32
  51.1 131.4 %collective-permute-start.5 = (bf16[2,3,2,256,512]{4,3,2,0,1:T(8,128)(2,1)}, bf16[2,3,2,256,512]{4,3,2,0,1:T(8,128)(2,1)}, u32[]{:S(2)}, u32[]{:S(2)}) collective-permute-start(bf16[2,3,2,256,512]{4,3,2,0,1:T(8,128)(2,1)} %pad_maximum_fusion.1), channel_id=1, source_target_pairs={{0,256},{256,0},{32,288},{288,32},{64,320},{320,64},{96,352},{352,... | collective-permute-start | bytes 9437192 | tf_op jit(solution)/shard_map/ppermute | solution.py:32
  174.9 1.2 copy-start.11
  174.9 2.1 %copy-start.13 = (bf16[2,1,1,2,256,512]{5,4,3,2,0,1:T(8,128)(2,1)S(1)}, bf16[2,1,1,2,256,512]{5,4,3,2,0,1:T(8,128)(2,1)}, u32[]{:S(2)}) copy-start(bf16[2,1,1,2,256,512]{5,4,3,2,0,1:T(8,128)(2,1)} %get-tuple-element.30) | copy-start | bytes 3145732
  174.9 2.6 %copy-start.19 = (f32[2,256,256]{2,1,0:T(8,128)S(1)}, f32[2,256,256]{2,1,0:T(8,128)}, u32[]{:S(2)}) copy-start(f32[2,256,256]{2,1,0:T(8,128)} %get-tuple-element.68) | copy-start | bytes 1572868
  175.3 5.5 %copy-start = (bf16[2,3,2,256,512]{4,3,2,0,1:T(8,128)(2,1)}, bf16[2,3,2,256,512]{4,3,2,0,1:T(8,128)(2,1)S(1)}, u32[]{:S(2)}) copy-start(bf16[2,3,2,256,512]{4,3,2,0,1:T(8,128)(2,1)S(1)} %copy_select_fusion.1) | copy-start | bytes 9437188
  177.5 1.6 copy-start.18
  179.1 1.7 copy-start.17
  188.8 1.2 copy-start.10
  188.9 1.5 copy-start.12
  188.9 1.7 copy-start.16
  190.5 1.0 copy-start.15
  191.6 1.0 copy-start.14
  192.6 0.9 copy-start.7
  192.6 1.0 copy-start.8
  192.6 1.1 copy-start.9
  193.4 1.9 copy-start.1
  193.7 2.3 %copy-start.4 = (bf16[2,1,1,256,256]{4,3,2,0,1:T(8,128)(2,1)S(1)}, bf16[2,1,1,256,256]{4,3,2,0,1:T(8,128)(2,1)}, u32[]{:S(2)}) copy-start(bf16[2,1,1,256,256]{4,3,2,0,1:T(8,128)(2,1)} %get-tuple-element.44) | copy-start | bytes 786436
  193.7 2.3 %copy-start.5 = (bf16[2,1,1,256,256]{4,3,2,0,1:T(8,128)(2,1)S(1)}, bf16[2,1,1,256,256]{4,3,2,0,1:T(8,128)(2,1)}, u32[]{:S(2)}) copy-start(bf16[2,1,1,256,256]{4,3,2,0,1:T(8,128)(2,1)} %get-tuple-element.45) | copy-start | bytes 786436
  193.7 2.3 %copy-start.6 = (bf16[2,1,1,256,256]{4,3,2,0,1:T(8,128)(2,1)S(1)}, bf16[2,1,1,256,256]{4,3,2,0,1:T(8,128)(2,1)}, u32[]{:S(2)}) copy-start(bf16[2,1,1,256,256]{4,3,2,0,1:T(8,128)(2,1)} %get-tuple-element.46) | copy-start | bytes 786436
  197.6 1.0 copy-start.2
  197.6 1.0 copy-start.3
where the time goes:
time: 203 us; the launch traced here: 202 us
  waiting for transfers between devices  123 us (61%)
  starting transfers between devices  29 us (14%)
  local copies, waits for them, and re-layouts  22.2 us (11%)
  other arithmetic  18.7 us (9%)
  matrix products  8.74 us (4%)
    ppermute x2, waiting for transfers between devices, swapped(): return lax.ppermute(block, axis, route)  112 us
    ppermute x2, starting transfers between devices, padded(): lax.ppermute(head, axis, [((i + 1) % count, i) for i in range(count)])  17.2 us
    ppermute x2, waiting for transfers between devices, padded(): lax.ppermute(head, axis, [((i + 1) % count, i) for i in range(count)])  8.92 us
    ppermute x2, starting transfers between devices, swapped(): return lax.ppermute(block, axis, route)  7.97 us
    ppermute x2, local copies, waits for them, and re-layouts, swapped(): return lax.ppermute(block, axis, route)  7.55 us
    concatenate x2, other arithmetic, padded(): jnp.concatenate([lax.ppermute(tail, axis, [(i, (i + 1) % count) for i in...  6.81 us
    unnamed x48, local copies, waits for them, and re-layouts  5.99 us
    gather x2, local copies, waits for them, and re-layouts, fetch_window(): extended = jnp.take(extended, slot_ids, axis=0)  5.27 us
  transfers between devices with their start and end apart: 6, of which 4 were waited for; matrix products, arithmetic and copies ran while one was open for 12% of the time, Pallas kernels for 0%

commit v1 on v0

v1 whole, which is shorter than its diff:
```python
import functools

import jax
import jax.numpy as jnp
from jax import lax
from jax.experimental import pallas as pl
from jax.experimental.pallas import tpu as pltpu
from jax.sharding import PartitionSpec as P

MESH = pl.DeviceIdType.MESH
scope = jax.named_scope
NT_DIMS = (((1,), (1,)), ((), ()))

UNIT = 128
CHUNKS = (
    ((0, 32), (32, 32), (64, 32), (96, 32), (128, 32), (160, 32), (192, 32), (224, 16), (240, 16)),
    ((0, 64), (64, 64), (128, 64), (192, 64)),
)
MOST = max(len(chunks) for chunks in CHUNKS)


def kernel(flips, factor_ref, partner_ref, occ_ref, sorted_ref, order_ref, out_ref, *scratch):
    nv = factor_ref.shape[4]
    naux = factor_ref.shape[5]
    halves = nv // UNIT
    windows = scratch[: 2 * halves * 3]
    (own, total, inverse, occ_s, partner_s, sorted_v, order_v,
     send_sems, recv_sems, own_sems, table_sems) = scratch[2 * halves * 3 :]
    window = lambda t, h, role: windows[(t * halves + h) * 3 + role]

    group = lax.axis_index("kpt")
    orbit = lax.axis_index("occ")
    orbits = lax.axis_size("occ")
    odd = lax.rem(orbit, 2)
    near = orbit + 1 - 2 * odd
    far = lax.rem(orbit + orbits - 1 + 2 * odd, orbits)
    partners = [(lax.bitwise_xor(group, 1 << flip), orbit) for flip in flips]
    early = lax.rem(group, 2) != orbit // (orbits // 2)
    near_id = (group, near)
    far_id = (group, far)

    tables = [
        pltpu.make_async_copy(src, dst, table_sems.at[n])
        for n, (src, dst) in enumerate(
            ((partner_ref, partner_s), (occ_ref, occ_s), (sorted_ref, sorted_v), (order_ref, order_v))
        )
    ]
    for copy in tables:
        copy.start()
    owns = []
    for t in (1, 0):
        for k in range(2):
            for n, (c, row, col) in enumerate(((0, 0, 0), (1, 0, 1), (1, 1, 0))):
                owns.append(
                    pltpu.make_async_copy(
                        factor_ref.at[t, k, 0, c],
                        own.at[t, k, pl.ds(row * nv, nv), pl.ds(col * naux, naux)],
                        own_sems.at[t, k, n],
                    )
                )
    for copy in owns:
        copy.start()

    half = orbits // 2
    bent = orbit // half != far // half
    bent_id = (partners[1][0], far)

    barrier = pltpu.get_barrier_semaphore()
    for target in (*partners, near_id, far_id):
        pl.semaphore_signal(barrier, inc=1, device_id=target, device_id_type=MESH)

    @pl.when(bent)
    def _():
        pl.semaphore_signal(barrier, inc=1, device_id=bent_id, device_id_type=MESH)

    with scope("barrier"):
        pl.semaphore_wait(barrier, 4 + bent.astype(jnp.int32))

    swaps, forwards = {}, {}
    for c in range(MOST):
        for t in range(2):
            if c < len(CHUNKS[t]):
                row, rows = CHUNKS[t][c]
                h, at = row // UNIT, row % UNIT
                here = window(t, h, 0).at[:, :, pl.ds(at, rows), :]
                swaps[t, c] = pltpu.make_async_remote_copy(
                    src_ref=factor_ref.at[t, :, 0, :, pl.ds(row, rows), :],
                    dst_ref=here,
                    send_sem=send_sems.at[0, t, c],
                    recv_sem=recv_sems.at[0, t, c],
                    device_id=partners[t],
                    device_id_type=MESH,
                )
                if t == 1:
                    straight = pltpu.make_async_remote_copy(
                        src_ref=factor_ref.at[t, :, 0, :, pl.ds(row, rows), :],
                        dst_ref=window(t, h, 2).at[:, :, pl.ds(at, rows), :],
                        send_sem=send_sems.at[2, t, c],
                        recv_sem=recv_sems.at[2, t, c],
                        device_id=bent_id,
                        device_id_type=MESH,
                    )
                    pl.when(bent)(straight.start)
                swaps[t, c].start()
                for role, target in ((2, far_id), (1, near_id)):
                    forwards[t, c, role] = pltpu.make_async_remote_copy(
                        src_ref=here,
                        dst_ref=window(t, h, role).at[:, :, pl.ds(at, rows), :],
                        send_sem=send_sems.at[role, t, c],
                        recv_sem=recv_sems.at[role, t, c],
                        device_id=target,
                        device_id_type=MESH,
                    )

    def take(t, *chunks):
        for c in chunks:
            with scope("take%d%d" % (t, c)):
                swaps[t, c].wait_recv()
                if t == 1:
                    pl.when(jnp.logical_not(bent))(forwards[t, c, 2].start)
                else:
                    forwards[t, c, 2].start()
                forwards[t, c, 1].start()

    def arrived(t, h, role):
        with scope("arrive%d%d%d" % (t, h, role)):
            for c, (row, _) in enumerate(CHUNKS[t]):
                if row // UNIT == h:
                    forwards[t, c, role].wait_recv()

    for copy in tables:
        copy.wait()
    for copy in owns:
        copy.wait()
    for t in range(2):
        for k in range(2):
            own[t, k, nv:, naux:] = -own[t, k, :nv, :naux]

    lane = lax.broadcasted_iota(jnp.int32, (nv, nv), 1)
    sub = lax.broadcasted_iota(jnp.int32, (nv, nv), 0)
    same = lane == sub

    def as_column(row, zero):
        return jnp.sum(jnp.where(same, row, zero), axis=1, keepdims=True)

    def virtual_row(k):
        ranks = order_v[pl.ds(k, 1), :]
        levels = as_column(sorted_v[pl.ds(k, 1), :], 0.0)
        return jnp.sum(jnp.where(ranks == sub, levels, 0.0), axis=0, keepdims=True)

    roles = (orbit, near, far)
    for k in range(2):
        own_k = group * 2 + k
        own_virtual = virtual_row(own_k)
        own_occ = occ_s[own_k, orbit]
        for t in range(2):
            point = partner_s[t, own_k]
            far_virtual = as_column(virtual_row(point), 0.0)
            for role in range(3):
                pair_occ = own_occ + occ_s[point, roles[role]]
                inverse[t, k, role] = 1.0 / ((pair_occ - far_virtual) - own_virtual)

    def part(t, h, k, role):
        slot = lax.rem(partner_s[t, group * 2 + k], 2)
        rows = window(t, h, role)[slot]
        side = jnp.concatenate([rows[0], rows[1]], axis=1)
        pair = lax.dot_general(own[t, k], side, NT_DIMS, preferred_element_type=jnp.float32)
        scale = inverse[t, k, role, :, h * UNIT : (h + 1) * UNIT]
        real = (pair[:nv] * scale).astype(jnp.bfloat16)
        imag = (pair[nv:] * scale).astype(jnp.bfloat16)
        mixed = jnp.concatenate(
            [jnp.concatenate([real, -imag], axis=1), jnp.concatenate([imag, real], axis=1)], axis=0
        )
        return mixed, rows.reshape(2 * UNIT, naux)

    def gradient(parts):
        mixed = jnp.concatenate([m for m, _ in parts], axis=1)
        rows = jnp.concatenate([r for _, r in parts], axis=0)
        return jnp.dot(mixed, rows, preferred_element_type=jnp.float32)

    def finish(t, k, value):
        out_ref[t, k, 0, 0] = value[:nv].astype(jnp.bfloat16)
        out_ref[t, k, 0, 1] = value[nv:].astype(jnp.bfloat16)

    def unit(t, h):
        for role in (1, 2):
            arrived(t, h, role)

        with scope("unit%d%d" % (t, h)):

            @pl.loop(0, 2)
            def _(k):
                value = gradient([part(t, h, k, role) for role in range(3)])
                if h == 0:
                    total[t, k] = value
                else:
                    finish(t, k, total[t, k] + value)

    def last(t, h):
        arrived(t, h, 1)
        with scope("near"):

            @pl.loop(0, 2)
            def _(k):
                total[t, k] += gradient([part(t, h, k, role) for role in range(2)])

        arrived(t, h, 2)
        with scope("far"):
            for k in range(2):
                finish(t, k, total[t, k] + gradient([part(t, h, k, 2)]))

    @pl.when(early)
    def _():
        for t, c in ((0, 0), (1, 0), (0, 1), (0, 2), (1, 1), (0, 3), (0, 4), (0, 5), (1, 2), (0, 6), (0, 7), (0, 8)):
            take(t, c)

    @pl.when(jnp.logical_not(early))
    def _():
        take(1, 0, 1, 2)

    unit(1, 0)
    take(1, 3)

    @pl.when(jnp.logical_not(early))
    def _():
        take(0, 0, 1)

    unit(1, 1)

    @pl.when(jnp.logical_not(early))
    def _():
        take(0, 2, 3, 4)

    @pl.when(jnp.logical_not(early) & bent)
    def _():
        take(0, 5, 6, 7, 8)

    unit(0, 0)

    @pl.when(jnp.logical_not(early | bent))
    def _():
        take(0, 5, 6, 7, 8)

    last(0, 1)

    with scope("drain"):
        for copy in (*swaps.values(), *forwards.values()):
            copy.wait_send()


def body(factor, partner, occ_energy, vir_sorted, vir_order):
    transfers, points, _, _, nv, naux = factor.shape
    top_bit = lax.axis_size("kpt").bit_length() - 2
    halves = nv // UNIT
    scratch = [pltpu.VMEM((points, 2, UNIT, naux), jnp.bfloat16)] * (transfers * halves * 3) + [
        pltpu.VMEM((transfers, points, 2 * nv, 2 * naux), jnp.bfloat16),
        pltpu.VMEM((transfers, points, 2 * nv, naux), jnp.float32),
        pltpu.VMEM((transfers, points, 3, nv, nv), jnp.float32),
        pltpu.SMEM(occ_energy.shape, jnp.float32),
        pltpu.SMEM(partner.shape, jnp.int32),
        pltpu.VMEM(vir_sorted.shape, jnp.float32),
        pltpu.VMEM(vir_order.shape, jnp.int32),
        pltpu.SemaphoreType.DMA((3, transfers, MOST)),
        pltpu.SemaphoreType.DMA((3, transfers, MOST)),
        pltpu.SemaphoreType.DMA((transfers, points, 3)),
        pltpu.SemaphoreType.DMA((4,)),
    ]
    return pl.pallas_call(
        functools.partial(kernel, (0, top_bit)),
        out_shape=jax.ShapeDtypeStruct(factor.shape, jnp.bfloat16),
        in_specs=[pl.BlockSpec(memory_space=pltpu.HBM)] * 5,
        out_specs=pl.BlockSpec(memory_space=pltpu.VMEM),
        scratch_shapes=scratch,
        compiler_params=pltpu.CompilerParams(
            collective_id=0, has_side_effects=True, vmem_limit_bytes=40 << 20
        ),
        name="exchange_contract",
    )(*(pltpu.with_memory_space_constraint(x, pltpu.HBM) for x in (factor, partner, occ_energy, vir_sorted, vir_order)))


def solution(mesh):
    in_specs = (P(None, "kpt", "occ", None, None, None), P(), P(), P(), P())
    out_specs = P(None, "kpt", "occ", None, None, None)
    return jax.shard_map(body, mesh=mesh, in_specs=in_specs, out_specs=out_specs, check_vma=False)
```

time: 203 us -> 70.5 us (0.35)
  the two profiles are of different devices: /device:TPU:6 before, /device:TPU:385 now
where the time goes in v1:
time: 70.5 us; the launch traced here: 70.4 us
  Pallas kernels  69 us (98%)
  local copies, waits for them, and re-layouts  1.32 us (2%)
    pallas_call x1, Pallas kernels, body(): pl.pallas_call(functools.partial(kernel, (0, top_bit)), out_shape=jax.Sha...  69 us

profile of v1, /device:TPU:385, one launch (start us, length us, event | category | flops | bytes accessed | tf_op | source)
XLA Modules:
  0.0 70.4 jit_solution(4814484352258573209)
XLA Ops:
  0.0 69.0 %exchange_contract.1 = bf16[2,2,1,2,256,512]{5,4,3,2,1,0:T(8,128)(2,1)S(1)} custom-call(bf16[2,2,1,2,256,512]{5,4,3,2,1,0:T(8,128)(2,1)} %factor_ref.1, s32[2,32]{1,0:T(2,128)} %partner_ref.1, f32[32,32]{1,0:T(8,128)} %occ_ref.1, f32[32,256]{1,0:T(8,128)} %sorted_ref.1, s32[32,256]{1,0:T(8,128)} %order_ref.1), custom_call_target="tpu_custom_call" | custom-call | tf_op jit(solution)/shard_map/exchange_contract/pallas_call | solution.py:268
  69.0 1.3 %copy.7 = bf16[2,2,1,2,256,512]{5,4,3,2,1,0:T(8,128)(2,1)} copy(bf16[2,2,1,2,256,512]{5,4,3,2,1,0:T(8,128)(2,1)S(1)} %exchange_contract.1) | data formatting | bytes 4194304

commit v2 on v1

--- a/solution.py
+++ b/solution.py
@@ -62,6 +62,7 @@
         copy.start()
 
     half = orbits // 2
+    hold = lax.rem(orbit + 2, half) == 0
     bent = orbit // half != far // half
     bent_id = (partners[1][0], far)
 
@@ -101,7 +102,7 @@
                         device_id_type=MESH,
                     )
                     pl.when(bent)(straight.start)
-                swaps[t, c].start()
+                    swaps[t, c].start()
                 for role, target in ((2, far_id), (1, near_id)):
                     forwards[t, c, role] = pltpu.make_async_remote_copy(
                         src_ref=here,
@@ -111,6 +112,12 @@
                         device_id=target,
                         device_id_type=MESH,
                     )
+
+    def send_first_transfer():
+        for c in range(len(CHUNKS[0])):
+            swaps[0, c].start()
+
+    pl.when(jnp.logical_not(hold))(send_first_transfer)
 
     def take(t, *chunks):
         for c in chunks:
@@ -158,25 +165,25 @@
             far_virtual = as_column(virtual_row(point), 0.0)
             for role in range(3):
                 pair_occ = own_occ + occ_s[point, roles[role]]
-                inverse[t, k, role] = 1.0 / ((pair_occ - far_virtual) - own_virtual)
-
-    def part(t, h, k, role):
+                value = 1.0 / ((pair_occ - far_virtual) - own_virtual)
+                for h in range(halves):
+                    columns = pl.ds(role * UNIT, UNIT)
+                    inverse[t, k, h, :, columns] = value[:, h * UNIT : (h + 1) * UNIT]
+
+    def gradient(t, h, k, roles):
         slot = lax.rem(partner_s[t, group * 2 + k], 2)
-        rows = window(t, h, role)[slot]
-        side = jnp.concatenate([rows[0], rows[1]], axis=1)
-        pair = lax.dot_general(own[t, k], side, NT_DIMS, preferred_element_type=jnp.float32)
-        scale = inverse[t, k, role, :, h * UNIT : (h + 1) * UNIT]
+        rows = [window(t, h, role)[slot] for role in roles]
+        reals = jnp.concatenate([r[0] for r in rows], axis=0)
+        imags = jnp.concatenate([r[1] for r in rows], axis=0)
+        sides = jnp.concatenate([reals, imags], axis=1)
+        pair = lax.dot_general(own[t, k], sides, NT_DIMS, preferred_element_type=jnp.float32)
+        scale = inverse[t, k, h, :, roles[0] * UNIT : (roles[-1] + 1) * UNIT]
         real = (pair[:nv] * scale).astype(jnp.bfloat16)
         imag = (pair[nv:] * scale).astype(jnp.bfloat16)
         mixed = jnp.concatenate(
             [jnp.concatenate([real, -imag], axis=1), jnp.concatenate([imag, real], axis=1)], axis=0
         )
-        return mixed, rows.reshape(2 * UNIT, naux)
-
-    def gradient(parts):
-        mixed = jnp.concatenate([m for m, _ in parts], axis=1)
-        rows = jnp.concatenate([r for _, r in parts], axis=0)
-        return jnp.dot(mixed, rows, preferred_element_type=jnp.float32)
+        return jnp.dot(mixed, jnp.concatenate([reals, imags], axis=0), preferred_element_type=jnp.float32)
 
     def finish(t, k, value):
         out_ref[t, k, 0, 0] = value[:nv].astype(jnp.bfloat16)
@@ -190,58 +197,61 @@
 
             @pl.loop(0, 2)
             def _(k):
-                value = gradient([part(t, h, k, role) for role in range(3)])
+                value = gradient(t, h, k, (0, 1, 2))
                 if h == 0:
                     total[t, k] = value
                 else:
                     finish(t, k, total[t, k] + value)
 
-    def last(t, h):
-        arrived(t, h, 1)
-        with scope("near"):
-
-            @pl.loop(0, 2)
-            def _(k):
-                total[t, k] += gradient([part(t, h, k, role) for role in range(2)])
-
-        arrived(t, h, 2)
-        with scope("far"):
-            for k in range(2):
-                finish(t, k, total[t, k] + gradient([part(t, h, k, 2)]))
+    late = jnp.logical_not(early)
+    late_straight = late & jnp.logical_not(bent)
 
     @pl.when(early)
     def _():
-        for t, c in ((0, 0), (1, 0), (0, 1), (0, 2), (1, 1), (0, 3), (0, 4), (0, 5), (1, 2), (0, 6), (0, 7), (0, 8)):
+        for t, c in ((0, 0), (1, 0), (0, 1), (0, 2), (1, 1), (0, 3), (0, 4), (0, 5)):
             take(t, c)
-
-    @pl.when(jnp.logical_not(early))
+        pl.when(hold)(send_first_transfer)
+        take(0, 6, 7, 8)
+        take(1, 2, 3)
+
+    @pl.when(late & bent)
     def _():
         take(1, 0, 1, 2)
+        take(0, 0, 1)
+        take(1, 3)
+        take(0, 2, 3)
+
+    @pl.when(late_straight)
+    def _():
+        take(1, 0)
+        pl.when(hold)(send_first_transfer)
+        take(1, 1, 2, 3)
+        pl.when(jnp.logical_not(hold))(lambda: take(0, 0, 1, 2, 3))
 
     unit(1, 0)
-    take(1, 3)
-
-    @pl.when(jnp.logical_not(early))
-    def _():
-        take(0, 0, 1)
+
+    @pl.when(late & bent)
+    def _():
+        take(0, 4, 5, 6, 7, 8)
+
+    @pl.when(late_straight & jnp.logical_not(hold))
+    def _():
+        take(0, 4)
 
     unit(1, 1)
 
-    @pl.when(jnp.logical_not(early))
-    def _():
-        take(0, 2, 3, 4)
-
-    @pl.when(jnp.logical_not(early) & bent)
-    def _():
-        take(0, 5, 6, 7, 8)
+    @pl.when(late_straight)
+    def _():
+        pl.when(hold)(lambda: take(0, 0, 1, 2, 3, 4))
+        take(0, 5, 6)
 
     unit(0, 0)
 
-    @pl.when(jnp.logical_not(early | bent))
-    def _():
-        take(0, 5, 6, 7, 8)
-
-    last(0, 1)
+    @pl.when(late_straight)
+    def _():
+        take(0, 7, 8)
+
+    unit(0, 1)
 
     with scope("drain"):
         for copy in (*swaps.values(), *forwards.values()):
@@ -255,7 +265,7 @@
     scratch = [pltpu.VMEM((points, 2, UNIT, naux), jnp.bfloat16)] * (transfers * halves * 3) + [
         pltpu.VMEM((transfers, points, 2 * nv, 2 * naux), jnp.bfloat16),
         pltpu.VMEM((transfers, points, 2 * nv, naux), jnp.float32),
-        pltpu.VMEM((transfers, points, 3, nv, nv), jnp.float32),
+        pltpu.VMEM((transfers, points, halves, nv, 3 * UNIT), jnp.float32),
         pltpu.SMEM(occ_energy.shape, jnp.float32),
         pltpu.SMEM(partner.shape, jnp.int32),
         pltpu.VMEM(vir_sorted.shape, jnp.float32),

time: 70.5 us -> 64.4 us (0.913)
  Pallas kernels: 69 us -> 63 us
    pallas_call x1, Pallas kernels: 69 us -> 63 us  [body(): pl.pallas_call(functools.partial(kernel, (0, top_bit)), out_shape=jax.Sha...]
where the time goes in v2:
time: 64.4 us; the launch traced here: 64.3 us
  Pallas kernels  63 us (98%)
  local copies, waits for them, and re-layouts  1.32 us (2%)
    pallas_call x1, Pallas kernels, body(): pl.pallas_call(functools.partial(kernel, (0, top_bit)), out_shape=jax.Sha...  63 us
    unnamed x1, local copies, waits for them, and re-layouts  1.32 us

profile of v2, /device:TPU:385, one launch (start us, length us, event | category | flops | bytes accessed | tf_op | source)
XLA Modules:
  0.0 64.3 jit_solution(3106436500192037268)
XLA Ops:
  0.0 63.0 %exchange_contract.1 = bf16[2,2,1,2,256,512]{5,4,3,2,1,0:T(8,128)(2,1)S(1)} custom-call(bf16[2,2,1,2,256,512]{5,4,3,2,1,0:T(8,128)(2,1)} %factor_ref.1, s32[2,32]{1,0:T(2,128)} %partner_ref.1, f32[32,32]{1,0:T(8,128)} %occ_ref.1, f32[32,256]{1,0:T(8,128)} %sorted_ref.1, s32[32,256]{1,0:T(8,128)} %order_ref.1), custom_call_target="tpu_custom_call" | custom-call | tf_op jit(solution)/shard_map/exchange_contract/pallas_call | solution.py:278
  63.0 1.3 %copy.7 = bf16[2,2,1,2,256,512]{5,4,3,2,1,0:T(8,128)(2,1)} copy(bf16[2,2,1,2,256,512]{5,4,3,2,1,0:T(8,128)(2,1)S(1)} %exchange_contract.1) | data formatting | bytes 4194304

commit v3 on v2

--- a/solution.py
+++ b/solution.py
@@ -77,47 +77,63 @@
     with scope("barrier"):
         pl.semaphore_wait(barrier, 4 + bent.astype(jnp.int32))
 
-    swaps, forwards = {}, {}
-    for c in range(MOST):
-        for t in range(2):
-            if c < len(CHUNKS[t]):
-                row, rows = CHUNKS[t][c]
-                h, at = row // UNIT, row % UNIT
-                here = window(t, h, 0).at[:, :, pl.ds(at, rows), :]
-                swaps[t, c] = pltpu.make_async_remote_copy(
-                    src_ref=factor_ref.at[t, :, 0, :, pl.ds(row, rows), :],
-                    dst_ref=here,
-                    send_sem=send_sems.at[0, t, c],
-                    recv_sem=recv_sems.at[0, t, c],
-                    device_id=partners[t],
+    swaps, forwards, straights = {}, {}, {}
+    for t in range(2):
+        for c, (row, rows) in enumerate(CHUNKS[t]):
+            h, at = row // UNIT, row % UNIT
+            source = factor_ref.at[t, :, 0, :, pl.ds(row, rows), :]
+            here, _, beyond = (window(t, h, role).at[:, :, pl.ds(at, rows), :] for role in range(3))
+            swaps[t, c] = pltpu.make_async_remote_copy(
+                src_ref=source,
+                dst_ref=here,
+                send_sem=send_sems.at[0, t, c],
+                recv_sem=recv_sems.at[0, t, c],
+                device_id=partners[t],
+                device_id_type=MESH,
+            )
+            if t == 1:
+                straights[c] = pltpu.make_async_remote_copy(
+                    src_ref=source,
+                    dst_ref=beyond,
+                    send_sem=send_sems.at[2, t, c],
+                    recv_sem=recv_sems.at[2, t, c],
+                    device_id=bent_id,
                     device_id_type=MESH,
                 )
-                if t == 1:
-                    straight = pltpu.make_async_remote_copy(
-                        src_ref=factor_ref.at[t, :, 0, :, pl.ds(row, rows), :],
-                        dst_ref=window(t, h, 2).at[:, :, pl.ds(at, rows), :],
-                        send_sem=send_sems.at[2, t, c],
-                        recv_sem=recv_sems.at[2, t, c],
-                        device_id=bent_id,
-                        device_id_type=MESH,
-                    )
-                    pl.when(bent)(straight.start)
-                    swaps[t, c].start()
-                for role, target in ((2, far_id), (1, near_id)):
-                    forwards[t, c, role] = pltpu.make_async_remote_copy(
-                        src_ref=here,
-                        dst_ref=window(t, h, role).at[:, :, pl.ds(at, rows), :],
-                        send_sem=send_sems.at[role, t, c],
-                        recv_sem=recv_sems.at[role, t, c],
-                        device_id=target,
-                        device_id_type=MESH,
-                    )
-
-    def send_first_transfer():
-        for c in range(len(CHUNKS[0])):
+            for role, target in ((2, far_id), (1, near_id)):
+                forwards[t, c, role] = pltpu.make_async_remote_copy(
+                    src_ref=here,
+                    dst_ref=window(t, h, role).at[:, :, pl.ds(at, rows), :],
+                    send_sem=send_sems.at[role, t, c],
+                    recv_sem=recv_sems.at[role, t, c],
+                    device_id=target,
+                    device_id_type=MESH,
+                )
+
+    slow = lax.rem(orbit + 3, half) == 0
+    after = early & (odd == 1) & jnp.logical_not(bent | slow)
+    final = len(CHUNKS[0]) - 2
+
+    def send_last_rows():
+        for c in range(final, final + 2):
             swaps[0, c].start()
 
-    pl.when(jnp.logical_not(hold))(send_first_transfer)
+    lead = 3
+
+    def send_lead():
+        for c in range(lead):
+            swaps[0, c].start()
+
+    def send_rest():
+        for c in range(lead, final):
+            swaps[0, c].start()
+        pl.when(jnp.logical_not(after))(send_last_rows)
+
+    pl.when(jnp.logical_not(hold & early))(send_lead)
+    pl.when(jnp.logical_not(hold))(send_rest)
+    for c in range(len(CHUNKS[1])):
+        pl.when(bent)(straights[c].start)
+        swaps[1, c].start()
 
     def take(t, *chunks):
         for c in chunks:
@@ -195,7 +211,7 @@
 
         with scope("unit%d%d" % (t, h)):
 
-            @pl.loop(0, 2)
+            @pl.loop(0, 2, unroll=(t, h) == (0, 1))
             def _(k):
                 value = gradient(t, h, k, (0, 1, 2))
                 if h == 0:
@@ -204,58 +220,62 @@
                     finish(t, k, total[t, k] + value)
 
     late = jnp.logical_not(early)
-    late_straight = late & jnp.logical_not(bent)
-
-    @pl.when(early)
+    plain = late & jnp.logical_not(bent | hold | slow)
+
+    @pl.when(early & jnp.logical_not(hold))
     def _():
         for t, c in ((0, 0), (1, 0), (0, 1), (0, 2), (1, 1), (0, 3), (0, 4), (0, 5)):
             take(t, c)
-        pl.when(hold)(send_first_transfer)
         take(0, 6, 7, 8)
         take(1, 2, 3)
 
+    @pl.when(early & hold)
+    def _():
+        for t, c in ((1, 0), (1, 1), (0, 0), (0, 1), (0, 2), (1, 2)):
+            take(t, c)
+        send_lead()
+        send_rest()
+        take(0, 3)
+        take(1, 3)
+        take(0, 4, 5, 6, 7, 8)
+
     @pl.when(late & bent)
     def _():
-        take(1, 0, 1, 2)
+        for t, c in ((1, 0), (0, 0), (0, 1), (1, 1), (0, 2), (0, 3), (1, 2), (0, 4), (0, 5), (1, 3)):
+            take(t, c)
+
+    @pl.when(late & jnp.logical_not(bent))
+    def _():
+        take(1, 0)
+        pl.when(hold)(send_rest)
+        take(1, 1, 2, 3)
         take(0, 0, 1)
-        take(1, 3)
-        take(0, 2, 3)
-
-    @pl.when(late_straight)
-    def _():
-        take(1, 0)
-        pl.when(hold)(send_first_transfer)
-        take(1, 1, 2, 3)
-        pl.when(jnp.logical_not(hold))(lambda: take(0, 0, 1, 2, 3))
+        pl.when(jnp.logical_not(hold))(lambda: take(0, 2, 3))
 
     unit(1, 0)
 
-    @pl.when(late & bent)
-    def _():
-        take(0, 4, 5, 6, 7, 8)
-
-    @pl.when(late_straight & jnp.logical_not(hold))
-    def _():
-        take(0, 4)
+    pl.when(late & slow)(lambda: take(0, 4, 5))
+    pl.when(late & (bent | slow))(lambda: take(0, 6, 7, 8))
+    pl.when(late & hold)(lambda: take(0, 2, 3))
+    pl.when(late & jnp.logical_not(bent | slow))(lambda: take(0, 4))
 
     unit(1, 1)
 
-    @pl.when(late_straight)
-    def _():
-        pl.when(hold)(lambda: take(0, 0, 1, 2, 3, 4))
-        take(0, 5, 6)
+    pl.when(late & hold)(lambda: take(0, 5, 6, 7, 8))
+    pl.when(plain)(lambda: take(0, 5))
 
     unit(0, 0)
 
-    @pl.when(late_straight)
-    def _():
-        take(0, 7, 8)
+    pl.when(plain)(lambda: take(0, 6, 7, 8))
 
     unit(0, 1)
 
     with scope("drain"):
-        for copy in (*swaps.values(), *forwards.values()):
-            copy.wait_send()
+        swaps[0, final - 1].wait_send()
+        pl.when(after)(send_last_rows)
+        for at, copy in (*swaps.items(), *forwards.items()):
+            if at != (0, final - 1):
+                copy.wait_send()
 
 
 def body(factor, partner, occ_energy, vir_sorted, vir_order):

time: 64.4 us -> 64.1 us (level)
  the two profiles are of different devices: /device:TPU:385 before, /device:TPU:16 now
where the time goes in v3:
time: 64.1 us; the launch traced here: 64 us
  Pallas kernels  62.7 us (98%)
  local copies, waits for them, and re-layouts  1.32 us (2%)
    pallas_call x1, Pallas kernels, body(): pl.pallas_call(functools.partial(kernel, (0, top_bit)), out_shape=jax.Sha...  62.7 us
    unnamed x1, local copies, waits for them, and re-layouts  1.32 us

profile of v3, /device:TPU:16, one launch (start us, length us, event | category | flops | bytes accessed | tf_op | source)
XLA Modules:
  0.0 64.0 jit_solution(2826825670557138838)
XLA Ops:
  0.0 62.7 %exchange_contract.1 = bf16[2,2,1,2,256,512]{5,4,3,2,1,0:T(8,128)(2,1)S(1)} custom-call(bf16[2,2,1,2,256,512]{5,4,3,2,1,0:T(8,128)(2,1)} %factor_ref.1, s32[2,32]{1,0:T(2,128)} %partner_ref.1, f32[32,32]{1,0:T(8,128)} %occ_ref.1, f32[32,256]{1,0:T(8,128)} %sorted_ref.1, s32[32,256]{1,0:T(8,128)} %order_ref.1), custom_call_target="tpu_custom_call" | custom-call | tf_op jit(solution)/shard_map/exchange_contract/pallas_call | solution.py:298
  62.7 1.3 %copy.7 = bf16[2,2,1,2,256,512]{5,4,3,2,1,0:T(8,128)(2,1)} copy(bf16[2,2,1,2,256,512]{5,4,3,2,1,0:T(8,128)(2,1)S(1)} %exchange_contract.1) | data formatting | bytes 4194304

commit v4 on v3

--- a/solution.py
+++ b/solution.py
@@ -112,10 +112,10 @@
 
     slow = lax.rem(orbit + 3, half) == 0
     after = early & (odd == 1) & jnp.logical_not(bent | slow)
-    final = len(CHUNKS[0]) - 2
+    final = len(CHUNKS[0]) - 3
 
     def send_last_rows():
-        for c in range(final, final + 2):
+        for c in range(final, final + 3):
             swaps[0, c].start()
 
     lead = 3
@@ -241,8 +241,10 @@
 
     @pl.when(late & bent)
     def _():
-        for t, c in ((1, 0), (0, 0), (0, 1), (1, 1), (0, 2), (0, 3), (1, 2), (0, 4), (0, 5), (1, 3)):
+        for t, c in ((1, 0), (0, 0), (0, 1), (1, 1), (0, 2), (0, 3), (1, 2), (0, 4), (0, 5)):
             take(t, c)
+        pl.when(odd == 1)(lambda: take(0, 6, 7, 8))
+        take(1, 3)
 
     @pl.when(late & jnp.logical_not(bent))
     def _():
@@ -255,7 +257,7 @@
     unit(1, 0)
 
     pl.when(late & slow)(lambda: take(0, 4, 5))
-    pl.when(late & (bent | slow))(lambda: take(0, 6, 7, 8))
+    pl.when(late & (bent & (odd == 0) | slow))(lambda: take(0, 6, 7, 8))
     pl.when(late & hold)(lambda: take(0, 2, 3))
     pl.when(late & jnp.logical_not(bent | slow))(lambda: take(0, 4))
 
@@ -263,10 +265,11 @@
 
     pl.when(late & hold)(lambda: take(0, 5, 6, 7, 8))
     pl.when(plain)(lambda: take(0, 5))
+    pl.when(plain & (odd == 0))(lambda: take(0, 6, 7, 8))
 
     unit(0, 0)
 
-    pl.when(plain)(lambda: take(0, 6, 7, 8))
+    pl.when(plain & (odd == 1))(lambda: take(0, 6, 7, 8))
 
     unit(0, 1)
 

time: 64.1 us -> 64.1 us (level)
  no operation moved by 1% of the time
where the time goes in v4:
time: 64.1 us; the launch traced here: 64 us
  Pallas kernels  62.7 us (98%)
  local copies, waits for them, and re-layouts  1.32 us (2%)
    pallas_call x1, Pallas kernels, body(): pl.pallas_call(functools.partial(kernel, (0, top_bit)), out_shape=jax.Sha...  62.7 us
    unnamed x1, local copies, waits for them, and re-layouts  1.32 us

profile of v4, /device:TPU:16, one launch (start us, length us, event | category | flops | bytes accessed | tf_op | source)
XLA Modules:
  0.0 64.0 jit_solution(17537013052397183356)
XLA Ops:
  0.0 62.7 %exchange_contract.1 = bf16[2,2,1,2,256,512]{5,4,3,2,1,0:T(8,128)(2,1)S(1)} custom-call(bf16[2,2,1,2,256,512]{5,4,3,2,1,0:T(8,128)(2,1)} %factor_ref.1, s32[2,32]{1,0:T(2,128)} %partner_ref.1, f32[32,32]{1,0:T(8,128)} %occ_ref.1, f32[32,256]{1,0:T(8,128)} %sorted_ref.1, s32[32,256]{1,0:T(8,128)} %order_ref.1), custom_call_target="tpu_custom_call" | custom-call | tf_op jit(solution)/shard_map/exchange_contract/pallas_call | solution.py:301
  62.7 1.3 %copy.7 = bf16[2,2,1,2,256,512]{5,4,3,2,1,0:T(8,128)(2,1)} copy(bf16[2,2,1,2,256,512]{5,4,3,2,1,0:T(8,128)(2,1)S(1)} %exchange_contract.1) | data formatting | bytes 4194304
